TPU v7x, 32 devices: a whole 2x2x4 slice. The times are simulated.
32 devices in a mesh: batch: 8 (over z, x), tensor: 4 (over y, core).
Axes of the slice: x: 2, y: 2, z: 4, core: 2. Of those that a mesh axis runs over, the one named last changes fastest.
Arguments:
- tokens: bfloat16 [2, 8192, 768], P(None, 'batch'), may hold values from -6 to 6
- lengths: int32 [2, 8, 1024], P(None, 'batch'), may hold values from 0 to 512, as said below
- quarters: int32 [2], replicated, may hold values from 1 to 4, as said below
- query_weight: bfloat16 [768, 768], P(None, 'tensor'), may hold values from -0.3125 to 0.3125
- query_bias: float32 [768], P('tensor'), may hold values from -4 to 4
- key_weight: bfloat16 [768, 768], P(None, 'tensor'), may hold values from -0.3125 to 0.3125
- value_weight: bfloat16 [768, 768], P(None, 'tensor'), may hold values from -0.21875 to 0.21875
- value_bias: float32 [768], P('tensor'), may hold values from -6 to 6
- out_weight: bfloat16 [768, 768], P('tensor'), may hold values from -0.625 to 0.625
- out_bias: float32 [768], replicated, may hold values from -6 to 6
- norm1_gain: float32 [768], replicated, may hold values from 0.5 to 1.5
- norm1_shift: float32 [768], replicated, may hold values from -4 to 4
- in_weight: bfloat16 [768, 3072], P(None, 'tensor'), may hold values from -0.21875 to 0.21875
- in_bias: float32 [3072], P('tensor'), may hold values from -6 to 6
- down_weight: bfloat16 [3072, 768], P('tensor'), may hold values from -0.109375 to 0.109375
- down_bias: float32 [768], replicated, may hold values from -6 to 6
- norm2_gain: float32 [768], replicated, may hold values from 0.5 to 1.5
- norm2_shift: float32 [768], replicated, may hold values from -4 to 4
- cotangent: bfloat16 [2, 8192, 768], P(None, 'batch'), may hold values from -6 to 6
Outputs:
- layer_out: bfloat16 [2, 8192, 768], P(None, ('batch', 'tensor'))
- input_grad: float32 [2, 8192, 768], P(None, ('batch', 'tensor'))
- query_weight_grad: float32 [768, 768], P(None, 'tensor')
- query_bias_grad: float32 [768], P('tensor')
- key_weight_grad: float32 [768, 768], P(None, 'tensor')
- value_weight_grad: float32 [768, 768], P(None, 'tensor')
- value_bias_grad: float32 [768], P('tensor')
- out_weight_grad: float32 [768, 768], P('tensor')
- out_bias_grad: float32 [768], replicated
- norm1_gain_grad: float32 [768], replicated
- norm1_shift_grad: float32 [768], replicated
- in_weight_grad: float32 [768, 3072], P(None, 'tensor')
- in_bias_grad: float32 [3072], P('tensor')
- down_weight_grad: float32 [3072, 768], P('tensor')
- down_bias_grad: float32 [768], replicated
- norm2_gain_grad: float32 [768], replicated
- norm2_shift_grad: float32 [768], replicated
Inputs may be any that keep to these rules, and one draw needn't show every extreme that they name: Row lengths[m, b] lists, in order, the lengths of the sequences packed into block b of micro-batch m; they sum to 1024, and 0 marks an unused slot. In every micro-batch one block holds a sequence of exactly 512 tokens. Micro-batch m keeps the first 12 * quarters[m] / 4 heads and the first 3072 * quarters[m] / 4 units; exactly one micro-batch has quarters 4.
All inputs are finite; a program needn't handle non-finite values.
Results may differ from a plain program's by a relative error of at most 0.013.
The roundings to bfloat16 on the way count: a program that leaves them out, or rounds other values in their place, can miss the bound.
Values may be sent and summed in bfloat16 or wider, within the bound.
A program may use at most 128 MiB of HBM per device.

v0:
```python
import jax
import jax.numpy as jnp
from jax import lax
from jax.sharding import PartitionSpec as P

HEADS = 12
HEAD_DIM = 64
FF = 3072
EPSILON = 1e-12
ROOT_HALF = 0.7071067811865476
DENSITY_SCALE = 0.3989422804014327


def layer_norm(values_in, gain, shift):
    row_mean = jnp.mean(values_in, axis=-1, keepdims=True)
    centred = values_in - row_mean
    inverse = lax.rsqrt(jnp.mean(centred * centred, axis=-1, keepdims=True) + EPSILON)
    normed = centred * inverse
    return (normed * gain + shift, normed, inverse)


def norm_back(grad_in, normed, inverse, gain):
    spread = grad_in * gain
    return inverse * (
        spread
        - jnp.mean(spread, axis=-1, keepdims=True)
        - normed * jnp.mean(spread * normed, axis=-1, keepdims=True)
    )


def gelu_slope(values_in):
    return (
        0.5 * (1.0 + lax.erf(values_in * ROOT_HALF))
        + values_in * jnp.exp(-0.5 * values_in * values_in) * DENSITY_SCALE
    )


def segment_of(slot_lengths):
    ends_at = jnp.cumsum(slot_lengths)
    places = jnp.arange(slot_lengths.shape[0], dtype=jnp.int32)
    return jnp.sum((ends_at[None, :] <= places[:, None]).astype(jnp.int32), axis=1)


def rows_of(array_in, row_first, row_share):
    return lax.dynamic_slice_in_dim(array_in, row_first, row_share, 0)


def cross_dot(left, right):
    return lax.dot_general(
        left, right, (((0,), (0,)), ((), ())), preferred_element_type=jnp.float32
    )


def back_dot(left, weight_in):
    return lax.dot_general(
        left, weight_in, (((1,), (1,)), ((), ())), preferred_element_type=jnp.float32
    )


def block_scores(query_block, key_heads, segment_block, segment):
    scores = (
        jnp.einsum("qhd,khd->hqk", query_block, key_heads, preferred_element_type=jnp.float32)
        * 0.125
    )
    return jnp.where((segment_block[:, None] == segment[None, :])[None], scores, -1e30)


def attend(queries, key_heads, value_heads, segment, block_rows):
    row_count, head_count, head_width = queries.shape
    block_count = row_count // block_rows

    def one_block(block_index):
        block_start = block_index * block_rows
        query_block = lax.dynamic_slice_in_dim(queries, block_start, block_rows, 0)
        segment_block = lax.dynamic_slice_in_dim(segment, block_start, block_rows, 0)
        scores = block_scores(query_block, key_heads, segment_block, segment)
        top_score = jnp.max(scores, axis=-1, keepdims=True)
        expo = jnp.exp(scores - top_score)
        totals = jnp.sum(expo, axis=-1, keepdims=True)
        probs_low = (expo / totals).astype(jnp.bfloat16)
        context = jnp.einsum(
            "hqk,khd->qhd", probs_low, value_heads, preferred_element_type=jnp.float32
        )
        return (context, (top_score + jnp.log(totals))[..., 0])

    context, log_total = lax.map(one_block, jnp.arange(block_count))
    return (context.reshape(row_count, head_count, head_width), log_total)


def attend_back(queries, key_heads, value_heads, segment, log_total, grad_context, block_rows):
    row_count, head_count, head_width = queries.shape
    block_count = row_count // block_rows

    def one_block(totals_in, block_index):
        key_total, value_total = totals_in
        block_start = block_index * block_rows
        query_block = lax.dynamic_slice_in_dim(queries, block_start, block_rows, 0)
        segment_block = lax.dynamic_slice_in_dim(segment, block_start, block_rows, 0)
        grad_block = lax.dynamic_slice_in_dim(grad_context, block_start, block_rows, 0)
        scores = block_scores(query_block, key_heads, segment_block, segment)
        probs = jnp.exp(scores - log_total[block_index][:, :, None])
        value_total = value_total + jnp.einsum(
            "hqk,qhd->khd",
            probs.astype(jnp.bfloat16),
            grad_block,
            preferred_element_type=jnp.float32,
        )
        grad_probs = jnp.einsum(
            "qhd,khd->hqk", grad_block, value_heads, preferred_element_type=jnp.float32
        )
        grad_scores = (
            probs * (grad_probs - jnp.sum(probs * grad_probs, axis=-1, keepdims=True))
        ).astype(jnp.bfloat16)
        query_grad = (
            jnp.einsum("hqk,khd->qhd", grad_scores, key_heads, preferred_element_type=jnp.float32)
            * 0.125
        )
        key_total = (
            key_total
            + jnp.einsum(
                "hqk,qhd->khd", grad_scores, query_block, preferred_element_type=jnp.float32
            )
            * 0.125
        )
        return ((key_total, value_total), query_grad)

    empty_grads = jnp.zeros((row_count, head_count, head_width), jnp.float32)
    (key_grad, value_grad), query_grads = lax.scan(
        one_block, (empty_grads, empty_grads), jnp.arange(block_count)
    )
    return (query_grads.reshape(row_count, head_count, head_width), key_grad, value_grad)


def local(
    tokens,
    lengths,
    quarters,
    query_weight,
    query_bias,
    key_weight,
    value_weight,
    value_bias,
    out_weight,
    out_bias,
    norm1_gain,
    norm1_shift,
    in_weight,
    in_bias,
    down_weight,
    down_bias,
    norm2_gain,
    norm2_shift,
    cotangent,
):
    group_count = lax.axis_size("tensor")
    tensor_place = lax.axis_index("tensor")
    micro_count, row_count, model_width = tokens.shape
    row_share = row_count // group_count
    row_first = tensor_place * row_share
    local_heads = query_weight.shape[1] // HEAD_DIM
    local_units = in_weight.shape[1]
    head_ids = tensor_place * local_heads + jnp.arange(local_heads, dtype=jnp.int32)
    unit_ids = tensor_place * local_units + jnp.arange(local_units, dtype=jnp.int32)
    block_rows = min(512, row_count)
    outputs = []
    input_grads = []
    split_terms = None
    shared_terms = None
    for micro_step in range(micro_count):
        live_quarter = quarters[micro_step]
        head_live = (4 * head_ids < HEADS * live_quarter).astype(jnp.float32)
        unit_live = (4 * unit_ids < FF * live_quarter).astype(jnp.float32)
        inputs = tokens[micro_step]
        segment = segment_of(lengths[micro_step, 0])
        queries = (
            jnp.dot(inputs, query_weight, preferred_element_type=jnp.float32) + query_bias
        ).astype(jnp.bfloat16)
        queries = queries.reshape(row_count, local_heads, HEAD_DIM)
        key_heads = jnp.dot(inputs, key_weight, preferred_element_type=jnp.float32).astype(
            jnp.bfloat16
        )
        key_heads = key_heads.reshape(row_count, local_heads, HEAD_DIM)
        value_heads = (
            jnp.dot(inputs, value_weight, preferred_element_type=jnp.float32) + value_bias
        ).astype(jnp.bfloat16)
        value_heads = value_heads.reshape(row_count, local_heads, HEAD_DIM)
        context, log_total = attend(queries, key_heads, value_heads, segment, block_rows)
        context_low = (
            (context * head_live[None, :, None])
            .astype(jnp.bfloat16)
            .reshape(row_count, local_heads * HEAD_DIM)
        )
        attn_partial = jnp.dot(context_low, out_weight, preferred_element_type=jnp.float32)
        inputs_wide = inputs.astype(jnp.float32)
        grad_out = cotangent[micro_step].astype(jnp.float32)
        grad_out_rows = rows_of(grad_out, row_first, row_share)
        attended = lax.psum(attn_partial, "tensor")
        hidden, normed_one, inverse_one = layer_norm(
            inputs_wide + attended + out_bias, norm1_gain, norm1_shift
        )
        hidden_low = hidden.astype(jnp.bfloat16)
        pre_act = jnp.dot(hidden_low, in_weight, preferred_element_type=jnp.float32) + in_bias
        active_low = (jax.nn.gelu(pre_act, approximate=False) * unit_live).astype(jnp.bfloat16)
        ffn_partial = jnp.dot(active_low, down_weight, preferred_element_type=jnp.float32)
        mixed = lax.psum(ffn_partial, "tensor")
        result_full, normed_two, inverse_two = layer_norm(
            hidden + mixed + down_bias, norm2_gain, norm2_shift
        )
        result_rows = rows_of(result_full, row_first, row_share)
        grad_mid2 = norm_back(grad_out, normed_two, inverse_two, norm2_gain)
        grad_mid2_rows = rows_of(grad_mid2, row_first, row_share)
        normed_two_rows = rows_of(normed_two, row_first, row_share)
        grad_mid2_low = grad_mid2.astype(jnp.bfloat16)
        outputs.append(result_rows.astype(jnp.bfloat16))
        norm2_gain_term = jnp.sum(grad_out_rows * normed_two_rows, axis=0)
        norm2_shift_term = jnp.sum(grad_out_rows, axis=0)
        down_bias_term = jnp.sum(grad_mid2_rows, axis=0)
        down_term = cross_dot(active_low, grad_mid2_low)
        grad_active = back_dot(grad_mid2_low, down_weight)
        grad_pre_low = (grad_active * unit_live * gelu_slope(pre_act)).astype(jnp.bfloat16)
        in_bias_term = jnp.sum(grad_pre_low.astype(jnp.float32), axis=0)
        in_term = cross_dot(hidden_low, grad_pre_low)
        hidden_partial = back_dot(grad_pre_low, in_weight)
        grad_hidden = grad_mid2 + lax.psum(hidden_partial, "tensor")
        grad_mid1 = norm_back(grad_hidden, normed_one, inverse_one, norm1_gain)
        grad_hidden_rows = rows_of(grad_hidden, row_first, row_share)
        normed_one_rows = rows_of(normed_one, row_first, row_share)
        grad_mid1_rows = rows_of(grad_mid1, row_first, row_share)
        grad_mid1_low = grad_mid1.astype(jnp.bfloat16)
        norm1_gain_term = jnp.sum(grad_hidden_rows * normed_one_rows, axis=0)
        norm1_shift_term = jnp.sum(grad_hidden_rows, axis=0)
        out_bias_term = jnp.sum(grad_mid1_rows, axis=0)
        out_term = cross_dot(context_low, grad_mid1_low)
        grad_context_low = (
            back_dot(grad_mid1_low, out_weight)
            .astype(jnp.bfloat16)
            .reshape(row_count, local_heads, HEAD_DIM)
        )
        grad_context_low = grad_context_low * head_live.astype(jnp.bfloat16)[None, :, None]
        grad_queries, grad_keys, grad_values = attend_back(
            queries, key_heads, value_heads, segment, log_total, grad_context_low, block_rows
        )
        grad_queries_low = grad_queries.astype(jnp.bfloat16).reshape(
            row_count, local_heads * HEAD_DIM
        )
        grad_keys_low = grad_keys.astype(jnp.bfloat16).reshape(row_count, local_heads * HEAD_DIM)
        grad_values_low = grad_values.astype(jnp.bfloat16).reshape(
            row_count, local_heads * HEAD_DIM
        )
        query_term = cross_dot(inputs, grad_queries_low)
        query_bias_term = jnp.sum(grad_queries_low.astype(jnp.float32), axis=0)
        key_term = cross_dot(inputs, grad_keys_low)
        value_term = cross_dot(inputs, grad_values_low)
        value_bias_term = jnp.sum(grad_values_low.astype(jnp.float32), axis=0)
        input_partial = (
            back_dot(grad_queries_low, query_weight)
            + back_dot(grad_keys_low, key_weight)
            + back_dot(grad_values_low, value_weight)
        )
        input_rows = (
            lax.psum_scatter(
                input_partial.astype(jnp.bfloat16), "tensor", scatter_dimension=0, tiled=True
            ).astype(jnp.float32)
            + grad_mid1_rows
        )
        input_grads.append(input_rows)
        new_split = (
            query_term,
            query_bias_term,
            key_term,
            value_term,
            value_bias_term,
            out_term,
            in_term,
            in_bias_term,
            down_term,
        )
        new_shared = (
            out_bias_term,
            norm1_gain_term,
            norm1_shift_term,
            down_bias_term,
            norm2_gain_term,
            norm2_shift_term,
        )
        if micro_step == 0:
            split_terms = new_split
            shared_terms = new_shared
        else:
            split_terms = jax.tree.map(jnp.add, split_terms, new_split)
            shared_terms = jax.tree.map(jnp.add, shared_terms, new_shared)
    (
        query_acc,
        query_bias_acc,
        key_acc,
        value_acc,
        value_bias_acc,
        out_acc,
        in_acc,
        in_bias_acc,
        down_acc,
    ) = split_terms
    (
        out_bias_acc,
        norm1_gain_acc,
        norm1_shift_acc,
        down_bias_acc,
        norm2_gain_acc,
        norm2_shift_acc,
    ) = shared_terms
    (
        query_sum,
        query_bias_sum,
        key_sum,
        value_sum,
        value_bias_sum,
        out_sum,
        in_sum,
        in_bias_sum,
        down_sum,
    ) = lax.psum(
        (
            query_acc,
            query_bias_acc,
            key_acc,
            value_acc,
            value_bias_acc,
            out_acc,
            in_acc,
            in_bias_acc,
            down_acc,
        ),
        "batch",
    )
    (
        out_bias_sum,
        norm1_gain_sum,
        norm1_shift_sum,
        down_bias_sum,
        norm2_gain_sum,
        norm2_shift_sum,
    ) = lax.psum(
        (
            out_bias_acc,
            norm1_gain_acc,
            norm1_shift_acc,
            down_bias_acc,
            norm2_gain_acc,
            norm2_shift_acc,
        ),
        ("batch", "tensor"),
    )
    return (
        jnp.stack(outputs),
        jnp.stack(input_grads),
        query_sum,
        query_bias_sum,
        key_sum,
        value_sum,
        value_bias_sum,
        out_sum,
        out_bias_sum,
        norm1_gain_sum,
        norm1_shift_sum,
        in_sum,
        in_bias_sum,
        down_sum,
        down_bias_sum,
        norm2_gain_sum,
        norm2_shift_sum,
    )


def solution(mesh):
    in_specs = (
        P(None, "batch", None),
        P(None, "batch", None),
        P(),
        P(None, "tensor"),
        P("tensor"),
        P(None, "tensor"),
        P(None, "tensor"),
        P("tensor"),
        P("tensor", None),
        P(),
        P(),
        P(),
        P(None, "tensor"),
        P("tensor"),
        P("tensor", None),
        P(),
        P(),
        P(),
        P(None, "batch", None),
    )
    out_specs = (
        P(None, ("batch", "tensor"), None),
        P(None, ("batch", "tensor"), None),
        P(None, "tensor"),
        P("tensor"),
        P(None, "tensor"),
        P(None, "tensor"),
        P("tensor"),
        P("tensor", None),
        P(),
        P(),
        P(),
        P(None, "tensor"),
        P("tensor"),
        P("tensor", None),
        P(),
        P(),
        P(),
    )
    return jax.shard_map(local, mesh=mesh, in_specs=in_specs, out_specs=out_specs, check_vma=False)
```

profile of v0, /device:TPU:0, one launch (start us, length us, event | category | flops | bytes accessed | tf_op | source)
XLA Modules:
  0.0 904.1 jit_solution(4392460739010797551)
XLA Ops:
  22.5 35.8 %while.54 = (s32[]{:T(128)}, f32[2,512,3,64]{1,0,3,2:T(2,128)}, f32[2,3,512]{2,1,0:T(4,128)}, s32[2]{0:T(128)}, s32[1024]{0:T(1024)S(1)}, /*index=5*/bf16[1024,3...) while((s32[]{:T(128)}, f32[2,512,3,64]{1,0,3,2:T(2,128)}, ...), condition=%wide.region_6.7_spmd, body=%wide.region_3.6_spmd.sunk | while | flops 422050304 | bytes 23982280 | solution.py:86
  28.3 3.1 fusion.333
  32.4 8.1 dynamic_update_slice.33
  46.0 3.1 fusion.333
  50.2 8.1 dynamic_update_slice.33
  63.0 32.8 %while.55 = (s32[]{:T(128)}, f32[2,512,3,64]{1,0,3,2:T(2,128)}, f32[2,3,512]{2,1,0:T(4,128)}, s32[2]{0:T(128)}, s32[1024]{0:T(1024)S(1)}, /*index=5*/bf16[1024,3...) while((s32[]{:T(128)}, f32[2,512,3,64]{1,0,3,2:T(2,128)}, ...), condition=%wide.region_19.20_spmd, body=%wide.region_16.19_spmd.sunk | while | flops 422050304 | bytes 24084736 | solution.py:86
  71.3 8.1 dynamic_update_slice.35
  87.6 8.1 dynamic_update_slice.35
  98.4 3.3 fusion.220
  106.0 120.6 %all-reduce.17.cloned.1.call-done = (f32[1024,768]{1,0:T(8,128)}, f32[1024,768]{1,0:T(8,128)}) async-done(((f32[1024,768]{1,0:T(8,128)}, f32[1024,768]{1,0:T(8,128)}), (f32[1024,768]{1,0:T(8,128)}, f32[1024,768]{1,0:T(8,128)})) %all-reduce.17.cloned.1.call-update) | async-done | bytes 6291472 | tf_op jit(solution)/shard_map/psum | solution.py:197
  226.6 4.8 fusion.180
  239.0 15.7 %fusion.73 = (bf16[1024,768]{1,0:T(8,128)(2,1)S(1)}, bf16[1024,768]{1,0:T(8,128)(2,1)S(1)}, f32[1024,768]{1,0:T(8,128)}) fusion(f32[768]{0:T(1024)S(1)} %fusion.217, f32[768]{0:T(1024)S(1)} %copy-done.86, f32[768]{0:T(1024)S(1)} %fusion.218, f32[1024,768]{1,0:T(8,128)S(1)} %fusion.195, bf16[768,768]{1,0:T(8,128)(2,1)S(1)} %copy-done, ...), kind=kOutput, calls=%fused_computation.95 | convolution fusion | flops 1315700736 | bytes 13777920 | tf_op jit(solution)/shard_map/dot_general | solution.py:202
  254.7 3.1 fusion.227
  257.8 3.1 fusion.228
  261.1 119.8 %all-reduce.15.cloned.1.call-done = (f32[1024,768]{1,0:T(8,128)}, f32[1024,768]{1,0:T(8,128)}) async-done(((f32[1024,768]{1,0:T(8,128)}, f32[1024,768]{1,0:T(8,128)}), (f32[1024,768]{1,0:T(8,128)}, f32[1024,768]{1,0:T(8,128)})) %all-reduce.15.cloned.1.call-update) | async-done | bytes 6291472 | tf_op jit(solution)/shard_map/psum | solution.py:205
  380.8 5.8 fusion.224
  396.6 3.0 convert_reduce_fusion.2
  399.6 3.1 fusion.232
  406.9 3.2 fusion.229
  410.2 4.0 fusion.191
  417.1 112.9 %all-reduce.13.cloned.1.call-done = (f32[1024,768]{1,0:T(8,128)}, f32[1024,768]{1,0:T(8,128)}) async-done(((f32[1024,768]{1,0:T(8,128)}, f32[1024,768]{1,0:T(8,128)}), (f32[1024,768]{1,0:T(8,128)}, f32[1024,768]{1,0:T(8,128)})) %all-reduce.13.cloned.1.call-update) | async-done | bytes 6291472 | tf_op jit(solution)/shard_map/psum | solution.py:224
  530.0 9.6 %multiply_reduce_fusion.11 = (f32[1024]{0:T(1024)S(1)}, f32[1024]{0:T(1024)S(1)}, f32[1024]{0:T(1024)S(1)}, f32[1024]{0:T(1024)S(1)}, f32[1024,768]{1,0:T(8,128)}, /*index=5*/f32[1024,768]{1,0:T(8,128)}) fusion(f32[768]{0:T(1024)S(1)} %copy-done.68, f32[1024,768]{1,0:T(8,128)} %copy-done.9, f32[1024,768]{1,0:T(8,128)} %copy-done.10, ...), kind=kLoop, calls=%fused_computation.175 | loop fusion | flops 7860224 | bytes 25185280 | tf_op jit(solution)/shard_map/reduce_sum | solution.py:26
  539.6 6.9 subtract_multiply_fusion.2
  549.2 29.8 %while.56 = (s32[]{:T(128)}, f32[1024,3,64]{0,2,1:T(8,128)S(1)}, f32[1024,3,64]{0,2,1:T(8,128)}, bf16[2,512,3,64]{1,3,2,0:T(8,128)(2,1)S(1)}, s32[2]{0:T(128)S(1...) while((s32[]{:T(128)}, f32[1024,3,64]{0,2,1:T(8,128)S(1)}, ...), condition=%wide.region_33.34_spmd.clone, body=%wide.region_31.33_spmd.clone.sunk | while | flops 1031830016 | bytes 61137236 | solution.py:128
  556.6 3.8 multiply_reduce_fusion.16
  571.5 3.8 multiply_reduce_fusion.16
  579.8 3.3 convolution_convert_fusion
  588.6 26.4 %while.57 = (s32[]{:T(128)}, f32[1024,3,64]{0,2,1:T(8,128)S(1)}, f32[1024,3,64]{0,2,1:T(8,128)}, bf16[2,512,3,64]{1,3,2,0:T(8,128)(2,1)}, s32[2]{0:T(128)S(1)}, ...) while((s32[]{:T(128)}, f32[1024,3,64]{0,2,1:T(8,128)S(1)}, ...), condition=%wide.region_42.43_spmd.clone, body=%wide.region_40.42_spmd.clone.sunk | while | flops 1031830016 | bytes 64283020 | solution.py:128
  620.2 4.0 fusion.197
  644.8 22.2 %all-reduce.1 = (f32[192]{0:T(256)}, f32[192]{0:T(256)}, f32[768]{0:T(1024)}) all-reduce(f32[192]{0:T(256)S(1)} %add.459, f32[192]{0:T(256)S(1)} %add.465, f32[768]{0:T(1024)S(1)} %add.471), channel_id=1, replica_groups=mesh['batch'=8,'tensor'=4] {'batch'}, use_global_device_ids=true, to_apply=%region_47.48 | all-reduce | flops 1152 | bytes 9216 | tf_op jit(solution)/shard_map/psum | solution.py:321
  669.7 40.9 %all-reduce = (f32[768]{0:T(1024)}, f32[768]{0:T(1024)}, f32[768]{0:T(1024)}, f32[768]{0:T(1024)}, f32[768]{0:T(1024)}, /*index=5*/f32[768]{0:T(1024)}) all-reduce(f32[768]{0:T(1024)S(1)} %add.467, f32[768]{0:T(1024)S(1)} %add.468, f32[768]{0:T(1024)S(1)} %add.469, ...), channel_id=1, replica_groups=mesh['batch'=8,'tensor'=4] {'batch','tensor'}, use_global_device_ids=true, to_apply=%region_56.57 | all-reduce | flops 4608 | bytes 36864 | tf_op jit(solution)/shard_map/psum | solution.py:342
  711.8 175.7 %all-reduce.11.cloned.1.call-done = (f32[768,192]{0,1:T(8,128)}, f32[768,192]{0,1:T(8,128)}, f32[768,192]{0,1:T(8,128)}, f32[192,768]{1,0:T(8,128)}, f32[768,768]{1,0:T(8,128)}, /*index=5*/f32[768,768]{1,0:T(8,128)}) async-done(((f32[768,192]{0,1:T(8,128)}, f32[768,192]{0,1:T(8,128)}, f32[768,192]{0,1:T(8,128)}, f32[192,768]{1,0:T(8,128)}, f32[768,768]{1,0:T(8,128)}, /*index=5*/f32[768,768]{1,0:T(8,128)}), ...) | async-done | bytes 7077904 | tf_op jit(solution)/shard_map/psum | solution.py:321
  (416 shorter events, 160.8 us)
Async XLA Ops:
  7.2 229.2 %copy-start = (bf16[768,768]{1,0:T(8,128)(2,1)S(1)}, bf16[768,768]{1,0:T(8,128)(2,1)}, u32[]{:S(2)}) copy-start(bf16[768,768]{1,0:T(8,128)(2,1)} %param.39) | copy-start | bytes 3538948
  7.2 219.4 %all-reduce.17.cloned.1.call-start = ((), (), s32[]{:S(2)}) async-start(), calls=%async_computation.7 | async-start | bytes 12582912 | tf_op jit(solution)/shard_map/psum | solution.py:197
  18.0 83.7 %copy-start.70 = (f32[192]{0:T(256)}, f32[192]{0:T(256)S(1)}, u32[]{:S(2)}) copy-start(f32[192]{0:T(256)S(1)} %mul.438) | copy-start | bytes 2308
  18.1 79.4 %copy-start.72 = (f32[192]{0:T(256)}, f32[192]{0:T(256)S(1)}, u32[]{:S(2)}) copy-start(f32[192]{0:T(256)S(1)} %mul.464) | copy-start | bytes 2308
  58.3 4.7 copy-start.4
  58.3 4.7 copy-start.20
  58.3 4.7 copy-start.53
  70.8 8.5 copy-start.63
  87.2 8.5 copy-start.63
  95.7 8.4 copy-start.2
  95.7 8.4 copy-start.18
  95.7 8.4 copy-start.27
  95.7 8.3 copy-start.51
  95.7 5.9 copy-start.29
  95.8 5.9 copy-start.33
  104.1 122.5 %copy-start.65 = (f32[768]{0:T(1024)S(1)}, f32[768]{0:T(1024)}, u32[]{:S(2)}) copy-start(f32[768]{0:T(1024)} %param.36) | copy-start | bytes 9220
  104.1 276.7 %all-reduce.15.cloned.1.call-start = ((), (), s32[]{:S(2)}) async-start(), calls=%async_computation.6 | async-start | bytes 12582912 | tf_op jit(solution)/shard_map/psum | solution.py:205
  226.6 4.8 copy-start.7
  226.6 5.6 copy-start.15
  226.6 6.5 copy-start.16
  238.0 16.7 %copy-start.92 = (f32[1024,768]{1,0:T(8,128)}, f32[1024,768]{1,0:T(8,128)S(1)}, u32[]{:S(2)}) copy-start(f32[1024,768]{1,0:T(8,128)S(1)} %fusion.195) | copy-start | bytes 9437188
  239.0 15.7 %copy-start.84 = (bf16[768,768]{1,0:T(8,128)(2,1)S(1)}, bf16[768,768]{1,0:T(8,128)(2,1)}, u32[]{:S(2)}) copy-start(bf16[768,768]{1,0:T(8,128)(2,1)} %param.41) | copy-start | bytes 3538948
  260.8 120.0 %copy-start.75 = (f32[768]{0:T(1024)S(1)}, f32[768]{0:T(1024)}, u32[]{:S(2)}) copy-start(f32[768]{0:T(1024)} %param.42) | copy-start | bytes 9220
  260.9 269.1 %all-reduce.13.cloned.1.call-start = ((), (), s32[]{:S(2)}) async-start(), calls=%async_computation.5 | async-start | bytes 12582912 | tf_op jit(solution)/shard_map/psum | solution.py:224
  391.1 5.5 copy-start.93
  394.2 5.4 copy-start.22
  394.2 8.5 copy-start.24
  410.1 256.9 %reduce-scatter.3.cloned.1.call-start = ((), (), s32[]{:S(2)}) async-start(), calls=%async_computation.2 | async-start | bytes 1966080 | tf_op jit(solution)/shard_map/reduce_scatter | solution.py:261
  586.6 81.7 %reduce-scatter.5.cloned.1.call-start = ((), (), s32[]{:S(2)}) async-start(), calls=%async_computation.3 | async-start | bytes 1966080 | tf_op jit(solution)/shard_map/reduce_scatter | solution.py:261
  619.9 267.6 %all-reduce.11.cloned.1.call-start = ((), (), s32[]{:S(2)}) async-start(), calls=%async_computation.4 | async-start | bytes 14155776 | tf_op jit(solution)/shard_map/psum | solution.py:321
  887.6 5.9 copy-start.61
  887.6 6.7 copy-start.42
  (80 other events, 200.7 us)
Sparse Core Ops, SparseCore 0:
  104.2 122.3 all-reduce.16
  261.0 119.8 all-reduce.14
  410.2 119.7 all-reduce.12
  586.7 28.2 reduce-scatter.2
  620.1 28.3 reduce-scatter.4
  654.5 232.9 all-reduce.10
where the time goes:
time: 911 us; the launch traced here: 904 us
  waiting for transfers between devices  529 us (58%)
  matrix products  128 us (14%)
  local copies, waits for them, and re-layouts  78.6 us (9%)
  other arithmetic  71.7 us (8%)
  blocking collectives  63 us (7%)
  between operations  18.2 us (2%)
  loops' own time  14.2 us (2%)
    psum x1, waiting for transfers between devices, local(): lax.psum((query_acc, query_bias_acc, key_acc, value_acc, value_bias_acc,...  176 us
    psum x1, waiting for transfers between devices, local(): attended = lax.psum(attn_partial, 'tensor')  121 us
    psum x1, waiting for transfers between devices, local(): mixed = lax.psum(ffn_partial, 'tensor')  120 us
    psum x1, waiting for transfers between devices, local(): grad_hidden = grad_mid2 + lax.psum(hidden_partial, 'tensor')  113 us
    psum x1, blocking collectives, local(): lax.psum((out_bias_acc, norm1_gain_acc, norm1_shift_acc, down_bias_acc, n...  40.9 us
    dynamic_update_slice x8, local copies, waits for them, and re-layouts, attend(): context, log_total = lax.map(one_block, jnp.arange(block_count))  33.9 us
    unnamed x190, local copies, waits for them, and re-layouts  26.4 us
    dot_general x12, matrix products, back_dot(): lax.dot_general(left, weight_in, (((1,), (1,)), ((), ())), preferred_elem...  22.4 us
  transfers between devices with their start and end apart: 6, of which 4 were waited for; matrix products, arithmetic and copies ran while one was open for 7% of the time, Pallas kernels for 0%

commit v1 on v0

--- a/solution.py
+++ b/solution.py
@@ -221,7 +221,7 @@
         in_bias_term = jnp.sum(grad_pre_low.astype(jnp.float32), axis=0)
         in_term = cross_dot(hidden_low, grad_pre_low)
         hidden_partial = back_dot(grad_pre_low, in_weight)
-        grad_hidden = grad_mid2 + lax.psum(hidden_partial, "tensor")
+        grad_hidden = grad_mid2 + jnp.sum(lax.all_gather(hidden_partial, "tensor"), axis=0)
         grad_mid1 = norm_back(grad_hidden, normed_one, inverse_one, norm1_gain)
         grad_hidden_rows = rows_of(grad_hidden, row_first, row_share)
         normed_one_rows = rows_of(normed_one, row_first, row_share)

time: 911 us -> 958 us (1.052)
  waiting for transfers between devices: 529 us -> 555 us
  other arithmetic: 71.7 us -> 88 us
    all_gather x0 -> x2, waiting for transfers between devices: none -> 139 us  [local(): lax.all_gather(hidden_partial, 'tensor')]
    psum x1 -> x0, waiting for transfers between devices: 113 us -> none  [local(): grad_hidden = grad_mid2 + lax.psum(hidden_partial, 'tensor')]
    reduce_sum x0 -> x2, other arithmetic: none -> 14.9 us  [local(): jnp.sum(lax.all_gather(hidden_partial, 'tensor'), axis=0)]
    unnamed x190 -> x186, local copies, waits for them, and re-layouts: 26.4 us -> 27.2 us
  transfers between devices with their start and end apart: 6 -> 7, of which waited for: 4 -> 5; matrix products, arithmetic and copies ran while one was open for 7% -> 8% of each run, Pallas kernels for 0% -> 0%
where the time goes in v1:
time: 958 us; the launch traced here: 951 us
  waiting for transfers between devices  555 us (58%)
  matrix products  132 us (14%)
  other arithmetic  88 us (9%)
  local copies, waits for them, and re-layouts  79.5 us (8%)
  blocking collectives  62.8 us (7%)
  between operations  18.2 us (2%)
  loops' own time  14 us (1%)
    psum x1, waiting for transfers between devices, local(): lax.psum((query_acc, query_bias_acc, key_acc, value_acc, value_bias_acc,...  176 us
    all_gather x2, waiting for transfers between devices, local(): lax.all_gather(hidden_partial, 'tensor')  139 us
    psum x1, waiting for transfers between devices, local(): attended = lax.psum(attn_partial, 'tensor')  121 us
    psum x1, waiting for transfers between devices, local(): mixed = lax.psum(ffn_partial, 'tensor')  120 us
    psum x1, blocking collectives, local(): lax.psum((out_bias_acc, norm1_gain_acc, norm1_shift_acc, down_bias_acc, n...  40.6 us
    dynamic_update_slice x8, local copies, waits for them, and re-layouts, attend(): context, log_total = lax.map(one_block, jnp.arange(block_count))  33.9 us
    unnamed x186, local copies, waits for them, and re-layouts  27.2 us
    dot_general x12, matrix products, back_dot(): lax.dot_general(left, weight_in, (((1,), (1,)), ((), ())), preferred_elem...  25.4 us
  transfers between devices with their start and end apart: 7, of which 5 were waited for; matrix products, arithmetic and copies ran while one was open for 8% of the time, Pallas kernels for 0%

profile of v1, /device:TPU:0, one launch (start us, length us, event | category | flops | bytes accessed | tf_op | source)
XLA Modules:
  0.0 951.1 jit_solution(3184664620574709415)
XLA Ops:
  22.5 35.8 %while.54 = (s32[]{:T(128)}, f32[2,512,3,64]{1,0,3,2:T(2,128)}, f32[2,3,512]{2,1,0:T(4,128)}, s32[2]{0:T(128)}, s32[1024]{0:T(1024)S(1)}, /*index=5*/bf16[1024,3...) while((s32[]{:T(128)}, f32[2,512,3,64]{1,0,3,2:T(2,128)}, ...), condition=%wide.region_6.7_spmd, body=%wide.region_3.6_spmd.sunk | while | flops 422050304 | bytes 23982280 | solution.py:86
  28.3 3.1 fusion.333
  32.4 8.1 dynamic_update_slice.33
  46.0 3.1 fusion.333
  50.2 8.1 dynamic_update_slice.33
  62.9 32.7 %while.55 = (s32[]{:T(128)}, f32[2,512,3,64]{1,0,3,2:T(2,128)}, f32[2,3,512]{2,1,0:T(4,128)}, s32[2]{0:T(128)}, s32[1024]{0:T(1024)S(1)}, /*index=5*/bf16[1024,3...) while((s32[]{:T(128)}, f32[2,512,3,64]{1,0,3,2:T(2,128)}, ...), condition=%wide.region_19.20_spmd, body=%wide.region_16.19_spmd.sunk | while | flops 422050304 | bytes 24084736 | solution.py:86
  71.2 8.1 dynamic_update_slice.35
  87.6 8.1 dynamic_update_slice.35
  98.3 3.3 fusion.220
  106.0 120.6 %all-reduce.13.cloned.1.call-done = (f32[1024,768]{1,0:T(8,128)}, f32[1024,768]{1,0:T(8,128)}) async-done(((f32[1024,768]{1,0:T(8,128)}, f32[1024,768]{1,0:T(8,128)}), (f32[1024,768]{1,0:T(8,128)}, f32[1024,768]{1,0:T(8,128)})) %all-reduce.13.cloned.1.call-update) | async-done | bytes 6291472 | tf_op jit(solution)/shard_map/psum | solution.py:197
  226.6 4.8 fusion.180
  239.0 15.7 %fusion.73 = (bf16[1024,768]{1,0:T(8,128)(2,1)S(1)}, bf16[1024,768]{1,0:T(8,128)(2,1)S(1)}, f32[1024,768]{1,0:T(8,128)}) fusion(f32[768]{0:T(1024)S(1)} %fusion.217, f32[768]{0:T(1024)S(1)} %copy-done.85, f32[768]{0:T(1024)S(1)} %fusion.218, f32[1024,768]{1,0:T(8,128)S(1)} %fusion.195, bf16[768,768]{1,0:T(8,128)(2,1)S(1)} %copy-done, ...), kind=kOutput, calls=%fused_computation.95 | convolution fusion | flops 1315700736 | bytes 13777920 | tf_op jit(solution)/shard_map/dot_general | solution.py:202
  261.1 119.7 %all-reduce.11.cloned.1.call-done = (f32[1024,768]{1,0:T(8,128)}, f32[1024,768]{1,0:T(8,128)}) async-done(((f32[1024,768]{1,0:T(8,128)}, f32[1024,768]{1,0:T(8,128)}), (f32[1024,768]{1,0:T(8,128)}, f32[1024,768]{1,0:T(8,128)})) %all-reduce.11.cloned.1.call-update) | async-done | bytes 6291472 | tf_op jit(solution)/shard_map/psum | solution.py:205
  380.8 5.8 fusion.224
  403.9 6.1 convert_reduce_fusion.3
  411.1 3.1 fusion.229
  414.6 4.8 fusion.191
  423.3 63.0 %all-gather.7.cloned.1.call-done = f32[4096,768]{1,0:T(8,128)} async-done(((f32[1024,768]{1,0:T(8,128)}), f32[4096,768]{1,0:T(8,128)}) %all-gather.7.cloned.1.call-update) | async-done | bytes 12582928 | tf_op jit(solution)/shard_map/all_gather | solution.py:224
  486.2 7.4 reduce_sum.395
  493.7 76.1 %all-gather.5.cloned.1.call-done = f32[4096,768]{1,0:T(8,128)} async-done(((f32[1024,768]{1,0:T(8,128)}), f32[4096,768]{1,0:T(8,128)}) %all-gather.5.cloned.1.call-update) | async-done | bytes 12582928 | tf_op jit(solution)/shard_map/all_gather | solution.py:224
  569.8 7.5 reduce_sum.390
  577.3 9.5 multiply_reduce_fusion.11
  586.8 7.1 subtract_multiply_fusion.2
  596.4 29.8 %while.56 = (s32[]{:T(128)}, f32[1024,3,64]{0,2,1:T(8,128)S(1)}, f32[1024,3,64]{0,2,1:T(8,128)}, bf16[2,512,3,64]{1,3,2,0:T(8,128)(2,1)S(1)}, s32[2]{0:T(128)S(1...) while((s32[]{:T(128)}, f32[1024,3,64]{0,2,1:T(8,128)S(1)}, ...), condition=%wide.region_33.34_spmd.clone, body=%wide.region_31.33_spmd.clone.sunk | while | flops 1031830016 | bytes 61137236 | solution.py:128
  603.9 3.8 multiply_reduce_fusion.16
  618.8 3.8 multiply_reduce_fusion.16
  627.1 3.3 convolution_convert_fusion
  635.8 26.2 %while.57 = (s32[]{:T(128)}, f32[1024,3,64]{0,2,1:T(8,128)S(1)}, f32[1024,3,64]{0,2,1:T(8,128)}, bf16[2,512,3,64]{1,3,2,0:T(8,128)(2,1)}, s32[2]{0:T(128)S(1)}, ...) while((s32[]{:T(128)}, f32[1024,3,64]{0,2,1:T(8,128)S(1)}, ...), condition=%wide.region_42.43_spmd.clone, body=%wide.region_40.42_spmd.clone.sunk | while | flops 1031830016 | bytes 64283020 | solution.py:128
  667.2 4.0 fusion.197
  691.9 22.2 %all-reduce.1 = (f32[192]{0:T(256)}, f32[192]{0:T(256)}, f32[768]{0:T(1024)}) all-reduce(f32[192]{0:T(256)S(1)} %add.455, f32[192]{0:T(256)S(1)} %add.461, f32[768]{0:T(1024)S(1)} %add.467), channel_id=1, replica_groups=mesh['batch'=8,'tensor'=4] {'batch'}, use_global_device_ids=true, to_apply=%region_47.48 | all-reduce | flops 1152 | bytes 9216 | tf_op jit(solution)/shard_map/psum | solution.py:321
  716.9 40.6 %all-reduce = (f32[768]{0:T(1024)}, f32[768]{0:T(1024)}, f32[768]{0:T(1024)}, f32[768]{0:T(1024)}, f32[768]{0:T(1024)}, /*index=5*/f32[768]{0:T(1024)}) all-reduce(f32[768]{0:T(1024)S(1)} %add.463, f32[768]{0:T(1024)S(1)} %add.464, f32[768]{0:T(1024)S(1)} %add.465, ...), channel_id=1, replica_groups=mesh['batch'=8,'tensor'=4] {'batch','tensor'}, use_global_device_ids=true, to_apply=%region_56.57 | all-reduce | flops 4608 | bytes 36864 | tf_op jit(solution)/shard_map/psum | solution.py:342
  758.7 175.8 %all-reduce.9.cloned.1.call-done = (f32[768,192]{0,1:T(8,128)}, f32[768,192]{0,1:T(8,128)}, f32[768,192]{0,1:T(8,128)}, f32[192,768]{1,0:T(8,128)}, f32[768,768]{1,0:T(8,128)}, /*index=5*/f32[768,768]{1,0:T(8,128)}) async-done(((f32[768,192]{0,1:T(8,128)}, f32[768,192]{0,1:T(8,128)}, f32[768,192]{0,1:T(8,128)}, f32[192,768]{1,0:T(8,128)}, f32[768,768]{1,0:T(8,128)}, /*index=5*/f32[768,768]{1,0:T(8,128)}), ...) | async-done | bytes 7077904 | tf_op jit(solution)/shard_map/psum | solution.py:321
  (417 shorter events, 172.4 us)
Async XLA Ops:
  7.2 229.1 %copy-start = (bf16[768,768]{1,0:T(8,128)(2,1)S(1)}, bf16[768,768]{1,0:T(8,128)(2,1)}, u32[]{:S(2)}) copy-start(bf16[768,768]{1,0:T(8,128)(2,1)} %param.39) | copy-start | bytes 3538948
  7.2 219.4 %all-reduce.13.cloned.1.call-start = ((), (), s32[]{:S(2)}) async-start(), calls=%async_computation.8 | async-start | bytes 12582912 | tf_op jit(solution)/shard_map/psum | solution.py:197
  18.0 83.7 %copy-start.69 = (f32[192]{0:T(256)}, f32[192]{0:T(256)S(1)}, u32[]{:S(2)}) copy-start(f32[192]{0:T(256)S(1)} %mul.438) | copy-start | bytes 2308
  18.1 79.3 %copy-start.71 = (f32[192]{0:T(256)}, f32[192]{0:T(256)S(1)}, u32[]{:S(2)}) copy-start(f32[192]{0:T(256)S(1)} %mul.464) | copy-start | bytes 2308
  58.3 4.7 copy-start.20
  58.3 4.7 copy-start.52
  70.8 8.5 copy-start.62
  87.2 8.5 copy-start.62
  95.7 8.4 copy-start.2
  95.7 8.4 copy-start.18
  95.7 8.4 copy-start.26
  95.7 8.3 copy-start.50
  95.7 5.9 copy-start.28
  95.7 5.9 copy-start.32
  104.1 122.5 %copy-start.64 = (f32[768]{0:T(1024)S(1)}, f32[768]{0:T(1024)}, u32[]{:S(2)}) copy-start(f32[768]{0:T(1024)} %param.36) | copy-start | bytes 9220
  104.1 276.7 %all-reduce.11.cloned.1.call-start = ((), (), s32[]{:S(2)}) async-start(), calls=%async_computation.7 | async-start | bytes 12582912 | tf_op jit(solution)/shard_map/psum | solution.py:205
  226.6 4.8 copy-start.7
  226.6 5.6 copy-start.15
  226.6 6.5 copy-start.16
  238.1 16.6 %copy-start.91 = (f32[1024,768]{1,0:T(8,128)}, f32[1024,768]{1,0:T(8,128)S(1)}, u32[]{:S(2)}) copy-start(f32[1024,768]{1,0:T(8,128)S(1)} %fusion.195) | copy-start | bytes 9437188
  239.0 15.7 %copy-start.83 = (bf16[768,768]{1,0:T(8,128)(2,1)S(1)}, bf16[768,768]{1,0:T(8,128)(2,1)}, u32[]{:S(2)}) copy-start(bf16[768,768]{1,0:T(8,128)(2,1)} %param.41) | copy-start | bytes 3538948
  260.8 120.0 %copy-start.74 = (f32[768]{0:T(1024)S(1)}, f32[768]{0:T(1024)}, u32[]{:S(2)}) copy-start(f32[768]{0:T(1024)} %param.42) | copy-start | bytes 9220
  260.9 225.4 %all-gather.7.cloned.1.call-start = ((), (), s32[]{:S(2)}) async-start(), calls=%async_computation.5 | async-start | bytes 15728640 | tf_op jit(solution)/shard_map/all_gather | solution.py:224
  391.1 5.4 copy-start.92
  403.8 166.0 %all-gather.5.cloned.1.call-start = ((), (), s32[]{:S(2)}) async-start(), calls=%async_computation.4 | async-start | bytes 15728640 | tf_op jit(solution)/shard_map/all_gather | solution.py:224
  414.3 299.8 %reduce-scatter.3.cloned.1.call-start = ((), (), s32[]{:S(2)}) async-start(), calls=%async_computation.2 | async-start | bytes 1966080 | tf_op jit(solution)/shard_map/reduce_scatter | solution.py:261
  414.6 4.9 copy-start.23
  414.6 5.8 copy-start.90
  633.8 81.7 %reduce-scatter.5.cloned.1.call-start = ((), (), s32[]{:S(2)}) async-start(), calls=%async_computation.3 | async-start | bytes 1966080 | tf_op jit(solution)/shard_map/reduce_scatter | solution.py:261
  666.9 267.6 %all-reduce.9.cloned.1.call-start = ((), (), s32[]{:S(2)}) async-start(), calls=%async_computation.6 | async-start | bytes 14155776 | tf_op jit(solution)/shard_map/psum | solution.py:321
  934.5 5.9 copy-start.60
  934.5 6.7 copy-start.41
  (79 other events, 200.4 us)
Sparse Core Ops, SparseCore 0:
  104.2 122.3 all-reduce.12
  261.0 119.7 all-reduce.10
  403.9 82.2 all-gather.6
  487.7 82.0 all-gather.4
  634.0 28.0 reduce-scatter.2
  667.0 28.1 reduce-scatter.4
  701.5 232.9 all-reduce.8
